TPU v7x, 1024 devices: a whole 8x8x8 slice. The times are simulated.
1024 devices in a mesh: vel: 16 (over y, core), sx: 8 (over z), sy: 8 (over x).
Axes of the slice: x: 8, y: 8, z: 8, core: 2. Of those that a mesh axis runs over, the one named last changes fastest.
Arguments:
- scaled_population_table: float32 [64, 64, 32768], P('sx', 'sy', 'vel'), may hold values from 0 to 8, as said below
Outputs:
- advanced: float32 [64, 64, 32768], P('sx', 'sy', 'vel')
Inputs may be any that keep to these rules, and one draw needn't show every extreme that they name: `scaled_population_table`: every entry is positive.
All inputs are finite; a program needn't handle non-finite values.
Results may differ from a plain program's by a relative error of at most 0.0003.
Values sent between devices are 32-bit elements; how exact they have to be, the bound alone decides.
A program may use at most 32 MiB of HBM per device.

v0:
```python
import math

import jax
import jax.numpy as jnp
from jax import lax
from jax.sharding import PartitionSpec as P

KV = 32


vel_bound = 4.5
time_step = 0.25 / 4.5
baseline_collision_interval = 0.25
power_law_index = 0.81
diffusivity_ratio_coefficient = 2.0 / 3.0
highest = lax.Precision.HIGHEST


def extended(array, sides, width):
    for axis, dim in sides:
        peers, length = (lax.axis_size(axis), array.shape[dim])
        up = [(i, (i + 1) % peers) for i in range(peers)]
        down = [(j, i) for i, j in up]
        last = lax.slice_in_dim(array, length - width, length, axis=dim)
        initial = lax.slice_in_dim(array, 0, width, axis=dim)
        before = lax.ppermute(last, axis, up)
        after = lax.ppermute(initial, axis, down)
        array = jnp.concatenate([before, array, after], axis=dim)
    return array


def velocity_table(vel_index):
    levels = (vel_index // (KV * KV), vel_index // KV % KV, vel_index % KV)
    return tuple(
        ((2 * one_level + 1 - KV).astype(jnp.float32) * (vel_bound / KV) for one_level in levels)
    )


def quad_weight():
    return (2.0 * vel_bound / KV) ** 3 * (2.0 * math.pi) ** (-1.5)


def minmod(former, latter):
    return (
        0.5 * (jnp.sign(former) + jnp.sign(latter)) * jnp.minimum(jnp.abs(former), jnp.abs(latter))
    )


def flux_change(padded, velocity, along_axis):
    length = padded.shape[along_axis]
    behind = lax.slice_in_dim(padded, 0, length - 2, axis=along_axis)
    middle = lax.slice_in_dim(padded, 1, length - 1, axis=along_axis)
    ahead_cell = lax.slice_in_dim(padded, 2, length, axis=along_axis)
    slopes = minmod(middle - behind, ahead_cell - middle)
    face_low = lax.slice_in_dim(middle + 0.5 * slopes, 0, length - 3, axis=along_axis)
    face_high = lax.slice_in_dim(middle - 0.5 * slopes, 1, length - 2, axis=along_axis)
    fluxes = jnp.maximum(velocity, 0.0) * face_low + jnp.minimum(velocity, 0.0) * face_high
    return lax.slice_in_dim(fluxes, 1, length - 3, axis=along_axis) - lax.slice_in_dim(
        fluxes, 0, length - 4, axis=along_axis
    )


def surround(field):
    return extended(field, (("sx", 0), ("sy", 1)), 2)


def project(flattened, moment_basis):
    return lax.dot_general(flattened, moment_basis, (((1,), (1,)), ((), ())), precision=highest)


def cell_moment_values(inner_cells, particle_speeds, quadrature_weight):
    cells_x, cells_y, vel_count = inner_cells.shape
    flattened = inner_cells.reshape(cells_x * cells_y, vel_count)
    squares = (
        particle_speeds[0] * particle_speeds[0]
        + particle_speeds[1] * particle_speeds[1]
        + particle_speeds[2] * particle_speeds[2]
    )
    moment_basis = jnp.stack(
        [
            jnp.ones_like(particle_speeds[0]),
            particle_speeds[0],
            particle_speeds[1],
            particle_speeds[2],
            squares,
        ]
    )
    partial_sums = project(flattened, moment_basis) * quadrature_weight
    integrated_sums_list = lax.psum(partial_sums, "vel").reshape(cells_x, cells_y, 5)
    local_matter_amount = integrated_sums_list[..., 0:1]
    bulk_flow_components = tuple(
        (
            integrated_sums_list[..., column : column + 1] / local_matter_amount
            for column in (1, 2, 3)
        )
    )
    bulk_flow_norm_square = (
        bulk_flow_components[0] * bulk_flow_components[0]
        + bulk_flow_components[1] * bulk_flow_components[1]
        + bulk_flow_components[2] * bulk_flow_components[2]
    )
    kinetic_warmth_level = (
        integrated_sums_list[..., 4:5] / local_matter_amount - bulk_flow_norm_square
    ) / 3.0
    neighbour_displacement_list = [
        particle_speeds[column] - bulk_flow_components[column] for column in range(3)
    ]
    velocity_dispersion_width = (
        neighbour_displacement_list[0] * neighbour_displacement_list[0]
        + neighbour_displacement_list[1] * neighbour_displacement_list[1]
        + neighbour_displacement_list[2] * neighbour_displacement_list[2]
    )
    weighted = inner_cells * velocity_dispersion_width
    heat_part = jnp.stack(
        [jnp.sum(weighted * neighbour_displacement_list[column], axis=2) for column in range(3)],
        axis=-1,
    ) * (0.5 * quadrature_weight)
    heat_total = lax.psum(heat_part, "vel")
    energy_current_triple = tuple((heat_total[..., column : column + 1] for column in range(3)))
    return (
        local_matter_amount,
        kinetic_warmth_level,
        energy_current_triple,
        neighbour_displacement_list,
        velocity_dispersion_width,
    )


def advance_section(padded, particle_speeds, quadrature_weight):
    inner_cells = padded[2:-2, 2:-2]
    (
        local_matter_amount,
        kinetic_warmth_level,
        energy_current_triple,
        neighbour_displacement_list,
        velocity_dispersion_width,
    ) = cell_moment_values(inner_cells, particle_speeds, quadrature_weight)
    collision_rate_coefficient = (
        local_matter_amount
        * kinetic_warmth_level ** (1.0 - power_law_index)
        / baseline_collision_interval
    )
    gaussian_rest_profile = (
        local_matter_amount
        * kinetic_warmth_level ** (-1.5)
        * jnp.exp(-velocity_dispersion_width / (2.0 * kinetic_warmth_level))
    )
    directional_energy_current = (
        neighbour_displacement_list[0] * energy_current_triple[0]
        + neighbour_displacement_list[1] * energy_current_triple[1]
        + neighbour_displacement_list[2] * energy_current_triple[2]
    )
    shakhov_attractor_profile = gaussian_rest_profile * (
        1.0
        + (1.0 - diffusivity_ratio_coefficient)
        * directional_energy_current
        / (5.0 * local_matter_amount * kinetic_warmth_level * kinetic_warmth_level)
        * (velocity_dispersion_width / kinetic_warmth_level - 5.0)
    )
    transport = flux_change(padded[:, 2:-2], particle_speeds[0], 0) + flux_change(
        padded[2:-2, :], particle_speeds[1], 1
    )
    return inner_cells + time_step * (
        collision_rate_coefficient * (shakhov_attractor_profile - inner_cells) - transport
    )


def local(scaled_population_table):
    vel_count = scaled_population_table.shape[2]
    vel_index = lax.axis_index("vel") * vel_count + jnp.arange(vel_count, dtype=jnp.int32)
    particle_speeds = velocity_table(vel_index)
    quadrature_weight = quad_weight()
    sectioned = advance_section(
        surround(scaled_population_table), particle_speeds, quadrature_weight
    )
    finished = advance_section(surround(sectioned), particle_speeds, quadrature_weight)
    return 0.5 * scaled_population_table + 0.5 * finished


def solution(mesh):
    return jax.shard_map(
        local,
        mesh=mesh,
        in_specs=(P("sx", "sy", "vel"),),
        out_specs=P("sx", "sy", "vel"),
        check_vma=False,
    )
```

profile of v0, /device:TPU:1, one launch (start us, length us, event | category | flops | bytes accessed | tf_op | source)
XLA Modules:
  0.0 247.5 jit_solution(12828199560752080076)
XLA Ops:
  0.0 1.0 fusion.111
  1.0 17.9 %collective-permute-start.1 = (f32[2,8,2048]{2,1,0:T(8,128)S(1)}, f32[2,8,2048]{2,1,0:T(8,128)S(1)}, u32[]{:S(2)}, u32[]{:S(2)}) collective-permute-start(f32[2,8,2048]{2,1,0:T(8,128)S(1)} %get-tuple-element.30), channel_id=1, source_target_pairs={{8,0},{16,8},{24,16},{32,24},{40,32},{48,40},{56,48},{0,56},{9,1},... | collective-permute-start | bytes 393224 | tf_op jit(solution)/shard_map/ppermute | solution.py:27
  18.9 1.9 collective-permute-start
  21.3 0.5 fusion
  21.9 46.6 %psum.28 = f32[8,8,5]{1,0,2:T(8,128)S(1)} all-reduce(f32[8,8,5]{1,0,2:T(8,128)S(1)} %reshape.280), channel_id=1, replica_groups=mesh['vel'=16,'sx'=8,'sy'=8] {'vel'}, use_global_device_ids=true, to_apply=%region_0.1 | all-reduce | flops 320 | bytes 2560 | tf_op jit(solution)/shard_map/psum | solution.py:89
  69.0 45.7 %psum.29 = f32[8,8,3]{1,0,2:T(8,128)S(1)} all-reduce(f32[8,8,3]{1,0,2:T(8,128)S(1)} %maximum_multiply_fusion), channel_id=1, replica_groups=mesh['vel'=16,'sx'=8,'sy'=8] {'vel'}, use_global_device_ids=true, to_apply=%region_4.5 | all-reduce | flops 192 | bytes 1536 | tf_op jit(solution)/shard_map/psum | solution.py:118
  115.2 4.5 %collective-permute-start.3 = (f32[12,2,2048]{2,0,1:T(8,128)S(1)}, f32[12,2,2048]{2,0,1:T(8,128)S(1)}, u32[]{:S(2)}, u32[]{:S(2)}) collective-permute-start(f32[12,2,2048]{2,0,1:T(8,128)S(1)} %copy.35), channel_id=1, source_target_pairs={{1,0},{2,1},{3,2},{4,3},{5,4},{6,5},{7,6},{0,7},{9,8},{10,9},{11,1... | collective-permute-start | bytes 589832 | tf_op jit(solution)/shard_map/ppermute | solution.py:27
  119.7 1.9 collective-permute-start.2
  122.2 0.7 collective-permute-done.3
  123.1 4.9 %collective-permute-done.2 = f32[12,2,2048]{2,0,1:T(8,128)S(1)} collective-permute-done((f32[12,2,2048]{2,0,1:T(8,128)S(1)}, f32[12,2,2048]{2,0,1:T(8,128)S(1)}, u32[]{:S(2)}, u32[]{:S(2)}) %collective-permute-start.2) | collective-permute-done | bytes 196640 | tf_op jit(solution)/shard_map/ppermute | solution.py:26
  128.2 1.1 pad_maximum_fusion.12
  129.6 0.8 multiply_add_fusion
  130.4 0.5 convolution_multiply_fusion
  131.0 48.0 %psum.30 = f32[8,8,5]{1,0,2:T(8,128)S(1)} all-reduce(f32[8,8,5]{1,0,2:T(8,128)S(1)} %reshape.282), channel_id=1, replica_groups=mesh['vel'=16,'sx'=8,'sy'=8] {'vel'}, use_global_device_ids=true, to_apply=%region_5.6 | all-reduce | flops 320 | bytes 2560 | tf_op jit(solution)/shard_map/psum | solution.py:89
  179.5 45.7 %psum.31 = f32[8,8,3]{1,0,2:T(8,128)S(1)} all-reduce(f32[8,8,3]{1,0,2:T(8,128)S(1)} %maximum_multiply_fusion.1), channel_id=1, replica_groups=mesh['vel'=16,'sx'=8,'sy'=8] {'vel'}, use_global_device_ids=true, to_apply=%region_9.10 | all-reduce | flops 192 | bytes 1536 | tf_op jit(solution)/shard_map/psum | solution.py:118
  225.2 1.9 collective-permute-start.4
  227.2 4.6 %collective-permute-start.5 = (f32[2,8,2048]{2,1,0:T(8,128)S(1)}, f32[2,8,2048]{2,1,0:T(8,128)S(1)}, u32[]{:S(2)}, u32[]{:S(2)}) collective-permute-start(f32[2,8,2048]{2,1,0:T(8,128)S(1)} %get-tuple-element.28), channel_id=1, source_target_pairs={{8,0},{16,8},{24,16},{32,24},{40,32},{48,40},{56,48},{0,56},{9,1},... | collective-permute-start | bytes 393224 | tf_op jit(solution)/shard_map/ppermute | solution.py:27
  232.2 1.5 collective-permute-done.5
  234.1 1.9 collective-permute-start.7
  236.0 3.4 %collective-permute-start.6 = (f32[12,2,2048]{2,0,1:T(8,128)S(1)}, f32[12,2,2048]{2,0,1:T(8,128)S(1)}, u32[]{:S(2)}, u32[]{:S(2)}) collective-permute-start(f32[12,2,2048]{2,0,1:T(8,128)S(1)} %copy.40), channel_id=1, source_target_pairs={{0,1},{1,2},{2,3},{3,4},{4,5},{5,6},{6,7},{7,0},{8,9},{9,10},{10,1... | collective-permute-start | bytes 589832 | tf_op jit(solution)/shard_map/ppermute | solution.py:26
  240.1 1.1 collective-permute-done.7
  241.4 3.0 %collective-permute-done.6 = f32[12,2,2048]{2,0,1:T(8,128)S(1)} collective-permute-done((f32[12,2,2048]{2,0,1:T(8,128)S(1)}, f32[12,2,2048]{2,0,1:T(8,128)S(1)}, u32[]{:S(2)}, u32[]{:S(2)}) %collective-permute-start.6) | collective-permute-done | bytes 196640 | tf_op jit(solution)/shard_map/ppermute | solution.py:26
  244.5 1.1 pad_maximum_fusion.6
  245.9 1.6 add_multiply_fusion
  (45 shorter events, 5.4 us)
Async XLA Ops:
  0.0 21.3 %copy-start = (f32[8,8,2048]{2,1,0:T(8,128)S(1)}, f32[8,8,2048]{2,1,0:T(8,128)}, u32[]{:S(2)}) copy-start(f32[8,8,2048]{2,1,0:T(8,128)} %param.1) | copy-start | bytes 1572868
  1.0 113.7 %collective-permute-start.1 = (f32[2,8,2048]{2,1,0:T(8,128)S(1)}, f32[2,8,2048]{2,1,0:T(8,128)S(1)}, u32[]{:S(2)}, u32[]{:S(2)}) collective-permute-start(f32[2,8,2048]{2,1,0:T(8,128)S(1)} %get-tuple-element.30), channel_id=1, source_target_pairs={{8,0},{16,8},{24,16},{32,24},{40,32},{48,40},{56,48},{0,56},{9,1},... | collective-permute-start | bytes 393224 | tf_op jit(solution)/shard_map/ppermute | solution.py:27
  18.9 49.6 %collective-permute-start = (f32[2,8,2048]{2,1,0:T(8,128)S(1)}, f32[2,8,2048]{2,1,0:T(8,128)S(1)}, u32[]{:S(2)}, u32[]{:S(2)}) collective-permute-start(f32[2,8,2048]{2,1,0:T(8,128)S(1)} %get-tuple-element.31), channel_id=1, source_target_pairs={{0,8},{8,16},{16,24},{24,32},{32,40},{40,48},{48,56},{56,0},{1,9},... | collective-permute-start | bytes 393224 | tf_op jit(solution)/shard_map/ppermute | solution.py:26
  115.2 7.8 %collective-permute-start.3 = (f32[12,2,2048]{2,0,1:T(8,128)S(1)}, f32[12,2,2048]{2,0,1:T(8,128)S(1)}, u32[]{:S(2)}, u32[]{:S(2)}) collective-permute-start(f32[12,2,2048]{2,0,1:T(8,128)S(1)} %copy.35), channel_id=1, source_target_pairs={{1,0},{2,1},{3,2},{4,3},{5,4},{6,5},{7,6},{0,7},{9,8},{10,9},{11,1... | collective-permute-start | bytes 589832 | tf_op jit(solution)/shard_map/ppermute | solution.py:27
  119.7 8.3 %collective-permute-start.2 = (f32[12,2,2048]{2,0,1:T(8,128)S(1)}, f32[12,2,2048]{2,0,1:T(8,128)S(1)}, u32[]{:S(2)}, u32[]{:S(2)}) collective-permute-start(f32[12,2,2048]{2,0,1:T(8,128)S(1)} %copy.34), channel_id=1, source_target_pairs={{0,1},{1,2},{2,3},{3,4},{4,5},{5,6},{6,7},{7,0},{8,9},{9,10},{10,1... | collective-permute-start | bytes 589832 | tf_op jit(solution)/shard_map/ppermute | solution.py:26
  225.2 6.9 %collective-permute-start.4 = (f32[2,8,2048]{2,1,0:T(8,128)S(1)}, f32[2,8,2048]{2,1,0:T(8,128)S(1)}, u32[]{:S(2)}, u32[]{:S(2)}) collective-permute-start(f32[2,8,2048]{2,1,0:T(8,128)S(1)} %get-tuple-element.27), channel_id=1, source_target_pairs={{0,8},{8,16},{16,24},{24,32},{32,40},{40,48},{48,56},{56,0},{1,9},... | collective-permute-start | bytes 393224 | tf_op jit(solution)/shard_map/ppermute | solution.py:26
  227.2 6.5 %collective-permute-start.5 = (f32[2,8,2048]{2,1,0:T(8,128)S(1)}, f32[2,8,2048]{2,1,0:T(8,128)S(1)}, u32[]{:S(2)}, u32[]{:S(2)}) collective-permute-start(f32[2,8,2048]{2,1,0:T(8,128)S(1)} %get-tuple-element.28), channel_id=1, source_target_pairs={{8,0},{16,8},{24,16},{32,24},{40,32},{48,40},{56,48},{0,56},{9,1},... | collective-permute-start | bytes 393224 | tf_op jit(solution)/shard_map/ppermute | solution.py:27
  234.1 7.1 %collective-permute-start.7 = (f32[12,2,2048]{2,0,1:T(8,128)S(1)}, f32[12,2,2048]{2,0,1:T(8,128)S(1)}, u32[]{:S(2)}, u32[]{:S(2)}) collective-permute-start(f32[12,2,2048]{2,0,1:T(8,128)S(1)} %copy.41), channel_id=1, source_target_pairs={{1,0},{2,1},{3,2},{4,3},{5,4},{6,5},{7,6},{0,7},{9,8},{10,9},{11,1... | collective-permute-start | bytes 589832 | tf_op jit(solution)/shard_map/ppermute | solution.py:27
  236.0 8.3 %collective-permute-start.6 = (f32[12,2,2048]{2,0,1:T(8,128)S(1)}, f32[12,2,2048]{2,0,1:T(8,128)S(1)}, u32[]{:S(2)}, u32[]{:S(2)}) collective-permute-start(f32[12,2,2048]{2,0,1:T(8,128)S(1)} %copy.40), channel_id=1, source_target_pairs={{0,1},{1,2},{2,3},{3,4},{4,5},{5,6},{6,7},{7,0},{8,9},{9,10},{10,1... | collective-permute-start | bytes 589832 | tf_op jit(solution)/shard_map/ppermute | solution.py:26
where the time goes:
time: 252 us; the launch traced here: 248 us
  blocking collectives  186 us (74%)
  starting transfers between devices  38 us (15%)
  waiting for transfers between devices  11.7 us (5%)
  other arithmetic  8.03 us (3%)
  local copies, waits for them, and re-layouts  2.58 us (1%)
    psum x2, blocking collectives, cell_moment_values(): lax.psum(partial_sums, 'vel').reshape(cells_x, cells_y, 5)  94.6 us
    psum x2, blocking collectives, cell_moment_values(): heat_total = lax.psum(heat_part, 'vel')  91.4 us
    ppermute x4, starting transfers between devices, extended(): after = lax.ppermute(initial, axis, down)  28.8 us
    ppermute x4, starting transfers between devices, extended(): before = lax.ppermute(last, axis, up)  9.11 us
    ppermute x4, waiting for transfers between devices, extended(): before = lax.ppermute(last, axis, up)  8.26 us
  transfers between devices with their start and end apart: 8, of which 6 were waited for; matrix products, arithmetic and copies ran while one was open for 1% of the time, Pallas kernels for 0%

commit v1 on v0

v1 whole, which is shorter than its diff:
```python
import functools

import jax
import jax.numpy as jnp
from jax import lax
from jax.experimental import pallas as pl
from jax.experimental.pallas import tpu as pltpu
from jax.sharding import PartitionSpec as P

KV = 32
BOUND = 4.5
DT = 0.25 / 4.5
UNIT = BOUND / KV
WEIGHT = (2.0 * BOUND / KV) ** 3 * (2.0 * 3.141592653589793) ** (-1.5)
MESH = pl.DeviceIdType.MESH
HIGHEST = lax.Precision.HIGHEST
NC = 64
LANES = 128


def functional_table():
    index = lax.broadcasted_iota(jnp.int32, (8, 1024), 1)
    row = lax.broadcasted_iota(jnp.int32, (8, 1024), 0)
    b = (2 * (index // KV) + 1 - KV).astype(jnp.float32) * UNIT
    e = (2 * (index % KV) + 1 - KV).astype(jnp.float32) * UNIT
    one = jnp.ones_like(b)
    rest = b * b + e * e
    rows = (one, b, e, b * b, b * e, e * e, b * rest, e * rest)
    table = jnp.zeros_like(b)
    for position, value in enumerate(rows):
        table = jnp.where(row == position, value, table)
    return table * WEIGHT


def partial_sums(cells, table):
    halves = [
        lax.dot_general(
            table,
            cells[:, half * 1024 : (half + 1) * 1024],
            (((1,), (1,)), ((), ())),
            precision=HIGHEST,
            preferred_element_type=jnp.float32,
        )
        for half in range(2)
    ]
    return jnp.concatenate(halves, axis=1)


def cell_coefficients(sums_ref, n_vel):
    lane = lax.broadcasted_iota(jnp.int32, (8, LANES), 1)
    second = (lane >= NC).astype(jnp.float32)
    powers = [None] * 4
    for source in range(n_vel):
        level = (4 * source + 1 - KV) * UNIT + second * (2.0 * UNIT)
        term = sums_ref[source]
        for power in range(4):
            powers[power] = term if powers[power] is None else powers[power] + term
            term = term * level
    r0, r1, r2, r3 = (value + pltpu.roll(value, NC, 1) for value in powers)
    n = r0[0:1]
    ma, mb, me = r1[0:1], r0[1:2], r0[2:3]
    aa, ab, ae, bb, be, ee = r2[0:1], r1[1:2], r1[2:3], r0[3:4], r0[4:5], r0[5:6]
    ta = r3[0:1] + r1[3:4] + r1[5:6]
    tb = r2[1:2] + r0[6:7]
    te = r2[2:3] + r0[7:8]
    inv_n = 1.0 / n
    ua, ub, ue = ma * inv_n, mb * inv_n, me * inv_n
    energy = aa + bb + ee
    speed2 = ua * ua + ub * ub + ue * ue
    temp = (energy * inv_n - speed2) * (1.0 / 3.0)
    common = 2.0 * n * speed2 - energy
    qa = 0.5 * (ta - 2.0 * (ua * aa + ub * ab + ue * ae) + ua * common)
    qb = 0.5 * (tb - 2.0 * (ua * ab + ub * bb + ue * be) + ub * common)
    qe = 0.5 * (te - 2.0 * (ua * ae + ub * be + ue * ee) + ue * common)
    log_t = jnp.log(temp)
    inv_t = 1.0 / temp
    dt_rate = n * jnp.exp(0.19 * log_t) * (DT / 0.25)
    amp = dt_rate * n * jnp.exp(-1.5 * log_t)
    scale = (1.0 - 2.0 / 3.0) / 5.0 * inv_n * inv_t * inv_t
    return ua, ub, ue, inv_t, amp, 1.0 - dt_rate, qa * scale, qb * scale, qe * scale


def write_coefficients(sums_ref, rows_ref, coef_ref, n_vel):
    rows_ref[...] = jnp.zeros_like(rows_ref)
    for position, value in enumerate(cell_coefficients(sums_ref, n_vel)):
        rows_ref[position : position + 1, :] = value
    coef_ref[...] = rows_ref[...].T


def clamp(value, low, high):
    return jnp.minimum(jnp.maximum(value, low), high)


def upwind(behind2, behind, here, ahead):
    d = here - behind
    low, high = jnp.minimum(d, 0.0), jnp.maximum(d, 0.0)
    slope = clamp(ahead, low, high)
    slope_behind = clamp(behind2, low, high)
    return d + 0.5 * (slope - slope_behind)


def advance_row(x, field, low_ref, high_ref, coef_ref, sign, speeds_a, emit):
    row = lax.broadcasted_iota(jnp.int32, (8, LANES), 0)
    lane = lax.broadcasted_iota(jnp.int32, (8, LANES), 1)
    first, last = row == 0, row == 7
    ce = (2 * (lane % KV) + 1 - KV).astype(jnp.float32) * UNIT
    lane_b = (2 * (lane // KV) - 3).astype(jnp.float32) * UNIT
    cell = coef_ref[pl.ds(pl.multiple_of(x * 8, 8), 8), :]
    ua, ub, ue, inv_t, amp, keep, qa, qb, qe = (
        jnp.broadcast_to(cell[:, c : c + 1], (8, LANES)) for c in range(9)
    )
    half_t = 0.5 * inv_t
    se = ce - ue
    se2, seq = se * se, se * qe
    level = []
    for speed in speeds_a:
        sa = speed - ua
        level.append((amp * jnp.exp(-(sa * sa) * half_t), sa * sa * inv_t - 5.0, sa * qa))
    for s in range(8):
        cb = lane_b + (8 * s - 28) * UNIT
        sb = cb - ub
        square = sb * sb + se2
        gauss = jnp.exp(-square * half_t)
        ratio = square * inv_t
        heat = sb * qb + seq
        vb = jnp.abs(cb) * DT
        for t in range(2):
            lanes = pl.ds((8 * t + s) * LANES, LANES)
            height, ratio_a, heat_a = level[t]
            relaxed = height * gauss * (1.0 + (heat + heat_a) * (ratio + ratio_a))
            g = field[x + 2, :, lanes]
            gm = field[x + 2 - sign, :, lanes]
            gmm = field[x + 2 - 2 * sign, :, lanes]
            gp = field[x + 2 + sign, :, lanes]
            along_x = upwind(gm - gmm, gm, g, gp - g)
            lo = low_ref[x, :, lanes]
            hi = high_ref[x, :, lanes]
            back = pltpu.roll(jnp.where(last, lo, g), 1, 0)
            front = pltpu.roll(jnp.where(first, hi, g), 7, 0)
            if s >= 4:
                d = g - back
                edge = lo - pltpu.roll(lo, 1, 0)
                before = pltpu.roll(jnp.where(last, edge, d), 1, 0)
                along_y = upwind(before, back, g, front - g)
            else:
                d = g - front
                edge = hi - pltpu.roll(hi, 7, 0)
                before = pltpu.roll(jnp.where(first, edge, d), 7, 0)
                along_y = upwind(before, front, g, back - g)
            speed = jnp.abs(speeds_a[t]) * DT
            emit(lanes, keep * g + relaxed - (speed * along_x + vb * along_y))


def kernel(
    n_vel, n_x, n_y, f_hbm, out_hbm,
    field, field2, low, high, low2, high2, out_v,
    send1, send2, sums1, sums2, rows, coef,
    in_sem, out_sem, halo_send, halo_recv, sum_send, sum_recv,
):
    v, sx, sy = lax.axis_index("vel"), lax.axis_index("sx"), lax.axis_index("sy")
    up_x, down_x = lax.rem(sx + 1, n_x), lax.rem(sx + n_x - 1, n_x)
    up_y, down_y = lax.rem(sy + 1, n_y), lax.rem(sy + n_y - 1, n_y)
    sides = ({"sx": up_x}, {"sx": down_x}, {"sy": up_y}, {"sy": down_y})

    barrier = pltpu.get_barrier_semaphore()
    for side in sides:
        pl.semaphore_signal(barrier, inc=1, device_id=side, device_id_type=MESH)
    for j in range(1, n_vel):
        pl.semaphore_signal(
            barrier, inc=1, device_id={"vel": lax.rem(v + j, n_vel)}, device_id_type=MESH
        )
    load = pltpu.make_async_copy(f_hbm, field.at[pl.ds(2, 8)], in_sem)
    load.start()

    table = functional_table()
    speeds_a = [
        (4 * v + 2 * t + 1 - KV).astype(jnp.float32) * UNIT for t in range(2)
    ]
    sign = jnp.where(v >= n_vel // 2, 1, -1)

    def exchange(source, low_dst, high_dst, stage):
        copies = []
        parts = (
            (source.at[pl.ds(8, 2)], source.at[pl.ds(0, 2)]),
            (source.at[pl.ds(2, 2)], source.at[pl.ds(10, 2)]),
            (source.at[pl.ds(2, 8), pl.ds(6, 2)], low_dst.at[:, pl.ds(6, 2)]),
            (source.at[pl.ds(2, 8), pl.ds(0, 2)], high_dst.at[:, pl.ds(0, 2)]),
        )
        for i, ((src, dst), side) in enumerate(zip(parts, sides)):
            copy = pltpu.make_async_remote_copy(
                src_ref=src, dst_ref=dst,
                send_sem=halo_send.at[stage, i], recv_sem=halo_recv.at[stage, i],
                device_id=side, device_id_type=MESH,
            )
            copy.start()
            copies.append(copy)
        return copies

    def share(send, sums, stage):
        copies = []
        for j in range(1, n_vel):
            copy = pltpu.make_async_remote_copy(
                src_ref=send, dst_ref=sums.at[v],
                send_sem=sum_send.at[stage, j], recv_sem=sum_recv.at[stage, v],
                device_id={"vel": lax.rem(v + j, n_vel)}, device_id_type=MESH,
            )
            copy.start()
            copies.append(copy)
        return copies

    def gather(send, sums, stage):
        for j in range(1, n_vel):
            other = lax.rem(v + j, n_vel)
            pltpu.make_async_remote_copy(
                src_ref=send, dst_ref=sums.at[other],
                send_sem=sum_send.at[stage, j], recv_sem=sum_recv.at[stage, other],
                device_id={"vel": other}, device_id_type=MESH,
            ).wait_recv()

    load.wait()
    own = partial_sums(field[pl.ds(2, 8)].reshape(NC, 2048), table)
    send1[...] = own
    sums1[v] = own
    pl.semaphore_wait(barrier, 4 + n_vel - 1)
    started = share(send1, sums1, 0)
    halos = exchange(field, low, high, 0)
    gather(send1, sums1, 0)
    write_coefficients(sums1, rows, coef, n_vel)
    for copy in halos:
        copy.wait_recv()
    started += halos

    @pl.loop(0, 8)
    def _(x):
        def emit(lanes, value):
            field2[x + 2, :, lanes] = value

        advance_row(x, field, low, high, coef, sign, speeds_a, emit)

    halos = exchange(field2, low2, high2, 1)
    own = partial_sums(field2[pl.ds(2, 8)].reshape(NC, 2048), table)
    send2[...] = own
    sums2[v] = own
    started += share(send2, sums2, 1)
    gather(send2, sums2, 1)
    write_coefficients(sums2, rows, coef, n_vel)
    for copy in halos:
        copy.wait_recv()
    started += halos

    @pl.loop(0, 8)
    def _(x):
        def emit(lanes, value):
            out_v[x, :, lanes] = 0.5 * (field[x + 2, :, lanes] + value)

        advance_row(x, field2, low2, high2, coef, sign, speeds_a, emit)

    store = pltpu.make_async_copy(out_v, out_hbm, out_sem)
    store.start()
    for copy in started:
        copy.wait_send()
    store.wait()


def solution(mesh):
    n_vel, n_x, n_y = mesh.shape["vel"], mesh.shape["sx"], mesh.shape["sy"]

    def step(table):
        block = table.shape
        return pl.pallas_call(
            functools.partial(kernel, n_vel, n_x, n_y),
            out_shape=jax.ShapeDtypeStruct(block, jnp.float32),
            in_specs=[pl.BlockSpec(memory_space=pl.ANY)],
            out_specs=pl.BlockSpec(memory_space=pl.ANY),
            scratch_shapes=[
                pltpu.VMEM((12, 8, 2048), jnp.float32),
                pltpu.VMEM((12, 8, 2048), jnp.float32),
                pltpu.VMEM(block, jnp.float32),
                pltpu.VMEM(block, jnp.float32),
                pltpu.VMEM(block, jnp.float32),
                pltpu.VMEM(block, jnp.float32),
                pltpu.VMEM(block, jnp.float32),
                pltpu.VMEM((8, LANES), jnp.float32),
                pltpu.VMEM((8, LANES), jnp.float32),
                pltpu.VMEM((n_vel, 8, LANES), jnp.float32),
                pltpu.VMEM((n_vel, 8, LANES), jnp.float32),
                pltpu.VMEM((LANES, LANES), jnp.float32),
                pltpu.VMEM((LANES, LANES), jnp.float32),
                pltpu.SemaphoreType.DMA,
                pltpu.SemaphoreType.DMA,
                pltpu.SemaphoreType.DMA((2, 4)),
                pltpu.SemaphoreType.DMA((2, 4)),
                pltpu.SemaphoreType.DMA((2, n_vel)),
                pltpu.SemaphoreType.DMA((2, n_vel)),
            ],
            compiler_params=pltpu.CompilerParams(
                collective_id=0, has_side_effects=True
            ),
        )(table)

    return jax.shard_map(
        step,
        mesh=mesh,
        in_specs=(P("sx", "sy", "vel"),),
        out_specs=P("sx", "sy", "vel"),
        check_vma=False,
    )
```

time: 252 us -> 38.3 us (0.15); the launches traced: 248 us -> 38 us
  blocking collectives: 186 us -> 0 us
  starting transfers between devices: 38 us -> 0 us
  Pallas kernels: 0 us -> 36.2 us
  waiting for transfers between devices: 11.7 us -> 0 us
  other arithmetic: 8.03 us -> 0 us
    psum x4 -> x0, blocking collectives: 186 us -> none  [the longest x2 94.6 us: cell_moment_values(): lax.psum(partial_sums, 'vel').reshape(cells_x, cells_y, 5)]
    ppermute x8 -> x0, starting transfers between devices: 38 us -> none  [the longest x4 28.8 us: extended(): after = lax.ppermute(initial, axis, down)]
    pallas_call x0 -> x1, Pallas kernels: none -> 36.2 us  [step(): pl.pallas_call(functools.partial(kernel, n_vel, n_x, n_y), out_shape=jax....]
    ppermute x8 -> x0, waiting for transfers between devices: 11.7 us -> none  [the longest x4 8.26 us: extended(): before = lax.ppermute(last, axis, up)]
    add x7 -> x0, other arithmetic: 3.42 us -> none  [the longest x1 1.62 us: local(): return 0.5 * scaled_population_table + 0.5 * finished]
  transfers between devices with their start and end apart: 8 -> 0, of which waited for: 6 -> 0; matrix products, arithmetic and copies ran while one was open for 1% -> 0% of each run, Pallas kernels for 0% -> 0%
where the time goes in v1:
time: 38.3 us; the launch traced here: 38 us
  Pallas kernels  36.2 us (95%)
  local copies, waits for them, and re-layouts  1.87 us (5%)
    pallas_call x1, Pallas kernels, step(): pl.pallas_call(functools.partial(kernel, n_vel, n_x, n_y), out_shape=jax....  36.2 us
    unnamed x1, local copies, waits for them, and re-layouts  1.87 us

profile of v1, /device:TPU:1, one launch (start us, length us, event | category | flops | bytes accessed | tf_op | source)
XLA Modules:
  0.0 38.0 jit_solution(17069589878981267039)
XLA Ops:
  0.0 36.2 %shard_map.17 = f32[8,8,2048]{2,1,0:T(8,128)} custom-call(f32[8,8,2048]{2,1,0:T(8,128)} %f_hbm.1), custom_call_target="tpu_custom_call" | custom-call | tf_op jit(solution)/shard_map/pallas_call | solution.py:270
  36.2 1.9 %copy.3 = f32[8,8,2048]{2,1,0:T(8,128)} copy(f32[8,8,2048]{2,1,0:T(8,128)} %shard_map.17) | data formatting | bytes 1048576

commit v2 on v1

--- a/solution.py
+++ b/solution.py
@@ -152,114 +152,140 @@
 
 
 def kernel(
-    n_vel, n_x, n_y, f_hbm, out_hbm,
-    field, field2, low, high, low2, high2, out_v,
-    send1, send2, sums1, sums2, rows, coef,
-    in_sem, out_sem, halo_send, halo_recv, sum_send, sum_recv,
+    n_vel, n_x, n_y, f_hbm, out_v,
+    field, field2, low, high, low2, high2, mine, sums, rows, coef, total,
+    in_sem, send_sem, x_sem, y_sem, sum_sem,
 ):
     v, sx, sy = lax.axis_index("vel"), lax.axis_index("sx"), lax.axis_index("sy")
     up_x, down_x = lax.rem(sx + 1, n_x), lax.rem(sx + n_x - 1, n_x)
-    up_y, down_y = lax.rem(sy + 1, n_y), lax.rem(sy + n_y - 1, n_y)
-    sides = ({"sx": up_x}, {"sx": down_x}, {"sy": up_y}, {"sy": down_y})
-
-    barrier = pltpu.get_barrier_semaphore()
-    for side in sides:
-        pl.semaphore_signal(barrier, inc=1, device_id=side, device_id_type=MESH)
-    for j in range(1, n_vel):
-        pl.semaphore_signal(
-            barrier, inc=1, device_id={"vel": lax.rem(v + j, n_vel)}, device_id_type=MESH
-        )
+    up_y, down_y = {"sy": lax.rem(sy + 1, n_y)}, {"sy": lax.rem(sy + n_y - 1, n_y)}
+    upward = v >= n_vel // 2
+    sign = jnp.where(upward, 1, -1)
+    order = sorted(range(1, n_vel), key=lambda j: -min(j, n_vel - j))
+    others = [{"vel": lax.rem(v + j, n_vel)} for j in order]
+
     load = pltpu.make_async_copy(f_hbm, field.at[pl.ds(2, 8)], in_sem)
     load.start()
+    barrier = pltpu.get_barrier_semaphore()
+    near = others + [{"sx": up_x}, {"sx": down_x}, up_y, down_y]
+    for side in near:
+        pl.semaphore_signal(barrier, inc=1, device_id=side, device_id_type=MESH)
 
     table = functional_table()
     speeds_a = [
         (4 * v + 2 * t + 1 - KV).astype(jnp.float32) * UNIT for t in range(2)
     ]
-    sign = jnp.where(v >= n_vel // 2, 1, -1)
-
-    def exchange(source, low_dst, high_dst, stage):
-        copies = []
+
+    def send(src, dst, recv_sem, to):
+        pltpu.make_async_remote_copy(
+            src_ref=src, dst_ref=dst, send_sem=send_sem, recv_sem=recv_sem,
+            device_id=to, device_id_type=MESH,
+        ).start()
+
+    def wait(ref, sem):
+        pltpu.make_async_copy(ref, ref, sem).wait()
+
+    def exchange_x(source, stage):
+        upwind_to = {"sx": jnp.where(upward, up_x, down_x)}
+        other_to = {"sx": jnp.where(upward, down_x, up_x)}
         parts = (
-            (source.at[pl.ds(8, 2)], source.at[pl.ds(0, 2)]),
-            (source.at[pl.ds(2, 2)], source.at[pl.ds(10, 2)]),
-            (source.at[pl.ds(2, 8), pl.ds(6, 2)], low_dst.at[:, pl.ds(6, 2)]),
-            (source.at[pl.ds(2, 8), pl.ds(0, 2)], high_dst.at[:, pl.ds(0, 2)]),
+            (jnp.where(upward, 8, 2), jnp.where(upward, 0, 10), 2, upwind_to),
+            (jnp.where(upward, 2, 9), jnp.where(upward, 10, 1), 1, other_to),
         )
-        for i, ((src, dst), side) in enumerate(zip(parts, sides)):
-            copy = pltpu.make_async_remote_copy(
-                src_ref=src, dst_ref=dst,
-                send_sem=halo_send.at[stage, i], recv_sem=halo_recv.at[stage, i],
-                device_id=side, device_id_type=MESH,
-            )
-            copy.start()
-            copies.append(copy)
-        return copies
-
-    def share(send, sums, stage):
-        copies = []
-        for j in range(1, n_vel):
-            copy = pltpu.make_async_remote_copy(
-                src_ref=send, dst_ref=sums.at[v],
-                send_sem=sum_send.at[stage, j], recv_sem=sum_recv.at[stage, v],
-                device_id={"vel": lax.rem(v + j, n_vel)}, device_id_type=MESH,
-            )
-            copy.start()
-            copies.append(copy)
-        return copies
-
-    def gather(send, sums, stage):
-        for j in range(1, n_vel):
-            other = lax.rem(v + j, n_vel)
-            pltpu.make_async_remote_copy(
-                src_ref=send, dst_ref=sums.at[other],
-                send_sem=sum_send.at[stage, j], recv_sem=sum_recv.at[stage, other],
-                device_id={"vel": other}, device_id_type=MESH,
-            ).wait_recv()
+        for src, dst, size, to in parts:
+            send(source.at[pl.ds(src, size)], source.at[pl.ds(dst, size)], x_sem.at[stage], to)
+
+    def exchange_y(source, low_dst, high_dst, stage):
+        for t in range(2):
+            for positive in range(2):
+                lanes = pl.ds(1024 * t + 512 * positive, 512)
+                row, size = (6, 2) if positive else (7, 1)
+                send(
+                    source.at[pl.ds(2, 8), pl.ds(row, size), lanes],
+                    low_dst.at[:, pl.ds(row, size), lanes], y_sem.at[stage], up_y,
+                )
+                size = 1 if positive else 2
+                send(
+                    source.at[pl.ds(2, 8), pl.ds(0, size), lanes],
+                    high_dst.at[:, pl.ds(0, size), lanes], y_sem.at[stage], down_y,
+                )
+
+    def own_sums(source, stage):
+        value = partial_sums(source[pl.ds(2, 8)].reshape(NC, 2048), table)
+        mine[stage] = value
+        sums[stage, v] = value
+
+    def share(stage):
+        for to in others:
+            send(mine.at[stage], sums.at[stage, v], sum_sem.at[stage], to)
+
+    def gather(stage):
+        wait(total.at[pl.ds(0, n_vel - 1)], sum_sem.at[stage])
+        write_coefficients(sums.at[stage], rows, coef, n_vel)
+
+    def arrive_x(stage):
+        wait(total.at[pl.ds(0, 3 * 16)], x_sem.at[stage])
+
+    def arrive_y(stage):
+        wait(total.at[pl.ds(0, 3 * 16)], y_sem.at[stage])
+
+    def row_of(i):
+        return jnp.where(upward, i, 7 - i)
 
     load.wait()
-    own = partial_sums(field[pl.ds(2, 8)].reshape(NC, 2048), table)
-    send1[...] = own
-    sums1[v] = own
-    pl.semaphore_wait(barrier, 4 + n_vel - 1)
-    started = share(send1, sums1, 0)
-    halos = exchange(field, low, high, 0)
-    gather(send1, sums1, 0)
-    write_coefficients(sums1, rows, coef, n_vel)
-    for copy in halos:
-        copy.wait_recv()
-    started += halos
-
-    @pl.loop(0, 8)
-    def _(x):
+    own_sums(field, 0)
+    pl.semaphore_wait(barrier, len(near))
+    share(0)
+    exchange_x(field, 0)
+    exchange_y(field, low, high, 0)
+    arrive_x(0)
+    arrive_y(0)
+    gather(0)
+
+    def first_step(i):
+        x = row_of(i)
+
         def emit(lanes, value):
             field2[x + 2, :, lanes] = value
 
         advance_row(x, field, low, high, coef, sign, speeds_a, emit)
 
-    halos = exchange(field2, low2, high2, 1)
-    own = partial_sums(field2[pl.ds(2, 8)].reshape(NC, 2048), table)
-    send2[...] = own
-    sums2[v] = own
-    started += share(send2, sums2, 1)
-    gather(send2, sums2, 1)
-    write_coefficients(sums2, rows, coef, n_vel)
-    for copy in halos:
-        copy.wait_recv()
-    started += halos
-
-    @pl.loop(0, 8)
-    def _(x):
+    @pl.loop(0, 3)
+    def _(i):
+        first_step(lax.rem(i + 6, 8))
+
+    exchange_x(field2, 1)
+
+    @pl.loop(1, 6)
+    def _(i):
+        first_step(i)
+
+    exchange_y(field2, low2, high2, 1)
+    own_sums(field2, 1)
+    share(1)
+
+    def second_step(i):
+        x = row_of(i)
+
         def emit(lanes, value):
             out_v[x, :, lanes] = 0.5 * (field[x + 2, :, lanes] + value)
 
         advance_row(x, field2, low2, high2, coef, sign, speeds_a, emit)
 
-    store = pltpu.make_async_copy(out_v, out_hbm, out_sem)
-    store.start()
-    for copy in started:
-        copy.wait_send()
-    store.wait()
+    arrive_y(1)
+    gather(1)
+
+    @pl.loop(2, 7)
+    def _(i):
+        second_step(i)
+
+    arrive_x(1)
+
+    @pl.loop(0, 3)
+    def _(i):
+        second_step(lax.rem(i + 7, 8))
+
+    wait(total, send_sem)
 
 
 def solution(mesh):
@@ -267,11 +293,12 @@
 
     def step(table):
         block = table.shape
+        table = pltpu.with_memory_space_constraint(table, pltpu.HBM)
         return pl.pallas_call(
             functools.partial(kernel, n_vel, n_x, n_y),
             out_shape=jax.ShapeDtypeStruct(block, jnp.float32),
-            in_specs=[pl.BlockSpec(memory_space=pl.ANY)],
-            out_specs=pl.BlockSpec(memory_space=pl.ANY),
+            in_specs=[pl.BlockSpec(memory_space=pltpu.HBM)],
+            out_specs=pl.BlockSpec(memory_space=pltpu.VMEM),
             scratch_shapes=[
                 pltpu.VMEM((12, 8, 2048), jnp.float32),
                 pltpu.VMEM((12, 8, 2048), jnp.float32),
@@ -279,22 +306,21 @@
                 pltpu.VMEM(block, jnp.float32),
                 pltpu.VMEM(block, jnp.float32),
                 pltpu.VMEM(block, jnp.float32),
-                pltpu.VMEM(block, jnp.float32),
-                pltpu.VMEM((8, LANES), jnp.float32),
-                pltpu.VMEM((8, LANES), jnp.float32),
-                pltpu.VMEM((n_vel, 8, LANES), jnp.float32),
-                pltpu.VMEM((n_vel, 8, LANES), jnp.float32),
+                pltpu.VMEM((2, 8, LANES), jnp.float32),
+                pltpu.VMEM((2, n_vel, 8, LANES), jnp.float32),
                 pltpu.VMEM((LANES, LANES), jnp.float32),
                 pltpu.VMEM((LANES, LANES), jnp.float32),
+                pltpu.VMEM((2 * (6 * 16 + n_vel - 1), 8, LANES), jnp.float32),
                 pltpu.SemaphoreType.DMA,
                 pltpu.SemaphoreType.DMA,
-                pltpu.SemaphoreType.DMA((2, 4)),
-                pltpu.SemaphoreType.DMA((2, 4)),
-                pltpu.SemaphoreType.DMA((2, n_vel)),
-                pltpu.SemaphoreType.DMA((2, n_vel)),
+                pltpu.SemaphoreType.DMA((2,)),
+                pltpu.SemaphoreType.DMA((2,)),
+                pltpu.SemaphoreType.DMA((2,)),
             ],
             compiler_params=pltpu.CompilerParams(
-                collective_id=0, has_side_effects=True
+                collective_id=0,
+                has_side_effects=True,
+                vmem_limit_bytes=16 * 1024 * 1024,
             ),
         )(table)
 

time: 38.3 us -> 35.7 us (0.932)
  Pallas kernels: 36.2 us -> 34.8 us
  local copies, waits for them, and re-layouts: 1.87 us -> 0.8 us
    pallas_call x1, Pallas kernels: 36.2 us -> 34.8 us  [step(): pl.pallas_call(functools.partial(kernel, n_vel, n_x, n_y), out_shape=jax....]
    unnamed x1, local copies, waits for them, and re-layouts: 1.87 us -> 0.8 us
where the time goes in v2:
time: 35.7 us; the launch traced here: 35.6 us
  Pallas kernels  34.8 us (97%)
  local copies, waits for them, and re-layouts  0.8 us (2%)
    pallas_call x1, Pallas kernels, step(): pl.pallas_call(functools.partial(kernel, n_vel, n_x, n_y), out_shape=jax....  34.8 us
    unnamed x1, local copies, waits for them, and re-layouts  0.8 us

profile of v2, /device:TPU:1, one launch (start us, length us, event | category | flops | bytes accessed | tf_op | source)
XLA Modules:
  0.0 35.6 jit_solution(15510760374970473248)
XLA Ops:
  0.0 34.8 %shard_map.17 = f32[8,8,2048]{2,1,0:T(8,128)S(1)} custom-call(f32[8,8,2048]{2,1,0:T(8,128)} %f_hbm.1), custom_call_target="tpu_custom_call" | custom-call | tf_op jit(solution)/shard_map/pallas_call | solution.py:297
  34.8 0.8 %copy.3 = f32[8,8,2048]{2,1,0:T(8,128)} copy(f32[8,8,2048]{2,1,0:T(8,128)S(1)} %shard_map.17) | data formatting | bytes 1048576

commit v3 on v2

--- a/solution.py
+++ b/solution.py
@@ -32,18 +32,24 @@
     return table * WEIGHT
 
 
-def partial_sums(cells, table):
-    halves = [
-        lax.dot_general(
+def partial_sums(cells, table, first):
+    pieces = []
+    size = cells.shape[0]
+    for half in range(2):
+        value = lax.dot_general(
             table,
             cells[:, half * 1024 : (half + 1) * 1024],
             (((1,), (1,)), ((), ())),
             precision=HIGHEST,
             preferred_element_type=jnp.float32,
         )
-        for half in range(2)
-    ]
-    return jnp.concatenate(halves, axis=1)
+        before, after = first, NC - first - size
+        if before:
+            pieces.append(jnp.zeros((8, before), jnp.float32))
+        pieces.append(value)
+        if after:
+            pieces.append(jnp.zeros((8, after), jnp.float32))
+    return jnp.concatenate(pieces, axis=1)
 
 
 def cell_coefficients(sums_ref, n_vel):
@@ -154,22 +160,60 @@
 def kernel(
     n_vel, n_x, n_y, f_hbm, out_v,
     field, field2, low, high, low2, high2, mine, sums, rows, coef, total,
-    in_sem, send_sem, x_sem, y_sem, sum_sem,
+    in_sem, send_sem, x_sem, y_sem, sum_sem, go,
 ):
     v, sx, sy = lax.axis_index("vel"), lax.axis_index("sx"), lax.axis_index("sy")
-    up_x, down_x = lax.rem(sx + 1, n_x), lax.rem(sx + n_x - 1, n_x)
+    up_x, down_x = {"sx": lax.rem(sx + 1, n_x)}, {"sx": lax.rem(sx + n_x - 1, n_x)}
     up_y, down_y = {"sy": lax.rem(sy + 1, n_y)}, {"sy": lax.rem(sy + n_y - 1, n_y)}
     upward = v >= n_vel // 2
+    downward = v < n_vel // 2
     sign = jnp.where(upward, 1, -1)
+
+    def fold(i, n):
+        return jnp.where(i < n // 2, i, n + n // 2 - 1 - i)
+
+    corner = jnp.logical_and(sx == 0, sy == 0)
+    top = jnp.logical_and(corner, v == 0)
+
+    def rank_of(vel):
+        plain = 2 * fold(vel // 2, n_vel // 2) + 1 - lax.rem(vel, 2)
+        in_corner = jnp.where(vel == 0, n_vel - 1, plain - jnp.where(plain > 1, 1, 0))
+        return jnp.where(corner, in_corner, plain)
+
+    def side_above(side, plain):
+        there_x, there_y = side.get("sx", sx), side.get("sy", sy)
+        there = jnp.logical_and(jnp.logical_and(there_x == 0, there_y == 0), v == 0)
+        return jnp.logical_and(jnp.logical_or(plain, there), jnp.logical_not(top))
+
+    y_rank = fold(sy, n_y)
+    sides = tuple(
+        (side, side_above(side, plain), index)
+        for side, plain, index in (
+            (up_x, up_x["sx"] > sx, 1),
+            (down_x, down_x["sx"] > sx, 0),
+            (up_y, fold(up_y["sy"], n_y) > y_rank, 3),
+            (down_y, fold(down_y["sy"], n_y) > y_rank, 2),
+        )
+    )
+    higher = [above for _, above, _ in sides]
+    lower = [jnp.logical_not(above) for above in higher]
+    rank = rank_of(v)
     order = sorted(range(1, n_vel), key=lambda j: -min(j, n_vel - j))
     others = [{"vel": lax.rem(v + j, n_vel)} for j in order]
 
+    barrier = pltpu.get_barrier_semaphore()
+    for to, above, _ in sides:
+        @pl.when(above)
+        def _(to=to):
+            pl.semaphore_signal(barrier, inc=1, device_id=to, device_id_type=MESH)
+
+    for to in others:
+        @pl.when(rank_of(to["vel"]) > rank)
+        def _(to=to):
+            pl.semaphore_signal(barrier, inc=1, device_id=to, device_id_type=MESH)
+
     load = pltpu.make_async_copy(f_hbm, field.at[pl.ds(2, 8)], in_sem)
     load.start()
-    barrier = pltpu.get_barrier_semaphore()
-    near = others + [{"sx": up_x}, {"sx": down_x}, up_y, down_y]
-    for side in near:
-        pl.semaphore_signal(barrier, inc=1, device_id=side, device_id_type=MESH)
 
     table = functional_table()
     speeds_a = [
@@ -182,110 +226,177 @@
             device_id=to, device_id_type=MESH,
         ).start()
 
-    def wait(ref, sem):
-        pltpu.make_async_copy(ref, ref, sem).wait()
-
-    def exchange_x(source, stage):
-        upwind_to = {"sx": jnp.where(upward, up_x, down_x)}
-        other_to = {"sx": jnp.where(upward, down_x, up_x)}
-        parts = (
-            (jnp.where(upward, 8, 2), jnp.where(upward, 0, 10), 2, upwind_to),
-            (jnp.where(upward, 2, 9), jnp.where(upward, 10, 1), 1, other_to),
-        )
-        for src, dst, size, to in parts:
-            send(source.at[pl.ds(src, size)], source.at[pl.ds(dst, size)], x_sem.at[stage], to)
-
-    def exchange_y(source, low_dst, high_dst, stage):
+    def wait(tiles, sem):
+        pltpu.make_async_copy(
+            total.at[pl.ds(0, tiles)], total.at[pl.ds(0, tiles)], sem
+        ).wait()
+
+    def send_x(source, stage, rising):
+        to, sem = (up_x, x_sem.at[stage, 0]) if rising else (down_x, x_sem.at[stage, 1])
+        far, near = ((8, 0), (9, 1)) if rising else ((2, 10), (2, 10))
+
+        @pl.when(upward if rising else downward)
+        def _():
+            src, dst = far
+            send(source.at[pl.ds(src, 2)], source.at[pl.ds(dst, 2)], sem, to)
+
+        @pl.when(downward if rising else upward)
+        def _():
+            src, dst = near
+            send(source.at[pl.ds(src, 1)], source.at[pl.ds(dst, 1)], sem, to)
+
+    def arrive_x(stage, rising):
+        sem = x_sem.at[stage, 0 if rising else 1]
+
+        @pl.when(upward if rising else downward)
+        def _():
+            wait(2 * 16, sem)
+
+        @pl.when(downward if rising else upward)
+        def _():
+            wait(16, sem)
+
+    def send_y(source, dst, sem, start, count, rising):
         for t in range(2):
             for positive in range(2):
                 lanes = pl.ds(1024 * t + 512 * positive, 512)
-                row, size = (6, 2) if positive else (7, 1)
+                if rising:
+                    row, size = (6, 2) if positive else (7, 1)
+                else:
+                    row, size = 0, (1 if positive else 2)
                 send(
-                    source.at[pl.ds(2, 8), pl.ds(row, size), lanes],
-                    low_dst.at[:, pl.ds(row, size), lanes], y_sem.at[stage], up_y,
+                    source.at[pl.ds(2 + start, count), pl.ds(row, size), lanes],
+                    dst.at[pl.ds(start, count), pl.ds(row, size), lanes],
+                    sem, up_y if rising else down_y,
                 )
-                size = 1 if positive else 2
-                send(
-                    source.at[pl.ds(2, 8), pl.ds(0, size), lanes],
-                    high_dst.at[:, pl.ds(0, size), lanes], y_sem.at[stage], down_y,
-                )
-
-    def own_sums(source, stage):
-        value = partial_sums(source[pl.ds(2, 8)].reshape(NC, 2048), table)
-        mine[stage] = value
-        sums[stage, v] = value
-
-    def share(stage):
+
+    def exchange_y(source, low_dst, high_dst, sem, start, count):
+        send_y(source, low_dst, sem, start, count, True)
+        send_y(source, high_dst, sem, start, count, False)
+
+    def own_sums(source, slot, start, count):
+        cells = source[pl.ds(2 + start, count)].reshape(8 * count, 2048)
+        value = partial_sums(cells, table, 8 * start)
+        mine[slot] = value
+        sums[slot, v] = value
+
+    def share(slot):
         for to in others:
-            send(mine.at[stage], sums.at[stage, v], sum_sem.at[stage], to)
-
-    def gather(stage):
-        wait(total.at[pl.ds(0, n_vel - 1)], sum_sem.at[stage])
-        write_coefficients(sums.at[stage], rows, coef, n_vel)
-
-    def arrive_x(stage):
-        wait(total.at[pl.ds(0, 3 * 16)], x_sem.at[stage])
-
-    def arrive_y(stage):
-        wait(total.at[pl.ds(0, 3 * 16)], y_sem.at[stage])
-
-    def row_of(i):
-        return jnp.where(upward, i, 7 - i)
-
-    load.wait()
-    own_sums(field, 0)
-    pl.semaphore_wait(barrier, len(near))
-    share(0)
-    exchange_x(field, 0)
-    exchange_y(field, low, high, 0)
-    arrive_x(0)
-    arrive_y(0)
-    gather(0)
-
-    def first_step(i):
-        x = row_of(i)
-
+            send(mine.at[slot], sums.at[slot, v], sum_sem.at[slot], to)
+
+    def gather(slot):
+        wait(n_vel - 1, sum_sem.at[slot])
+        write_coefficients(sums.at[slot], rows, coef, n_vel)
+
+    def first_step(x):
         def emit(lanes, value):
             field2[x + 2, :, lanes] = value
 
         advance_row(x, field, low, high, coef, sign, speeds_a, emit)
 
-    @pl.loop(0, 3)
-    def _(i):
-        first_step(lax.rem(i + 6, 8))
-
-    exchange_x(field2, 1)
-
-    @pl.loop(1, 6)
-    def _(i):
-        first_step(i)
-
-    exchange_y(field2, low2, high2, 1)
-    own_sums(field2, 1)
-    share(1)
-
-    def second_step(i):
-        x = row_of(i)
-
+    def second_step(x):
         def emit(lanes, value):
             out_v[x, :, lanes] = 0.5 * (field[x + 2, :, lanes] + value)
 
         advance_row(x, field2, low2, high2, coef, sign, speeds_a, emit)
 
-    arrive_y(1)
+    begin = (
+        lambda: send_x(field, 0, True),
+        lambda: send_x(field, 0, False),
+        lambda: send_y(field, low, y_sem.at[0], 0, 8, True),
+        lambda: send_y(field, high, y_sem.at[0], 0, 8, False),
+    )
+    entered = sum(below.astype(jnp.int32) for below in lower) + rank
+
+    @pl.when(entered > 0)
+    def _():
+        pl.semaphore_wait(barrier, entered)
+
+    for (to, _, index), below in zip(sides, lower):
+        @pl.when(below)
+        def _(to=to, index=index):
+            pl.semaphore_signal(go.at[index], inc=1, device_id=to, device_id_type=MESH)
+
+    for to in others:
+        @pl.when(rank_of(to["vel"]) < rank)
+        def _(to=to):
+            pl.semaphore_signal(go.at[4], inc=1, device_id=to, device_id_type=MESH)
+
+    load.wait()
+    for start, below in zip(begin, lower):
+        pl.when(below)(start)
+
+    own_sums(field, 0, 0, 8)
+    for to in others:
+        @pl.when(rank_of(to["vel"]) < rank)
+        def _(to=to):
+            send(mine.at[0], sums.at[0, v], sum_sem.at[0], to)
+
+    def begin_above(index):
+        @pl.when(higher[index])
+        def _():
+            pl.semaphore_wait(go.at[index], 1)
+            begin[index]()
+
+    begin_above(2)
+    begin_above(3)
+    begin_above(0)
+
+    @pl.when(rank < n_vel - 1)
+    def _():
+        pl.semaphore_wait(go.at[4], n_vel - 1 - rank)
+
+    for to in others:
+        @pl.when(rank_of(to["vel"]) > rank)
+        def _(to=to):
+            send(mine.at[0], sums.at[0, v], sum_sem.at[0], to)
+
+    wait(3 * 16, y_sem.at[0])
+    gather(0)
+
+    @pl.loop(2, 6)
+    def _(x):
+        first_step(x)
+
+    begin_above(1)
+    arrive_x(0, False)
+
+    @pl.loop(6, 8)
+    def _(x):
+        first_step(x)
+
+    send_x(field2, 1, True)
+    own_sums(field2, 1, 2, 6)
+    share(1)
+    exchange_y(field2, low2, high2, y_sem.at[1], 2, 6)
+    arrive_x(0, True)
+
+    @pl.loop(0, 2)
+    def _(x):
+        first_step(x)
+
+    own_sums(field2, 2, 0, 2)
+    share(2)
+    send_x(field2, 1, False)
+    exchange_y(field2, low2, high2, y_sem.at[2], 0, 2)
+
+    wait(36, y_sem.at[1])
+    arrive_x(1, False)
     gather(1)
 
-    @pl.loop(2, 7)
-    def _(i):
-        second_step(i)
-
-    arrive_x(1)
-
-    @pl.loop(0, 3)
-    def _(i):
-        second_step(lax.rem(i + 7, 8))
-
-    wait(total, send_sem)
+    @pl.loop(2, 8)
+    def _(x):
+        second_step(x)
+
+    wait(12, y_sem.at[2])
+    arrive_x(1, True)
+    gather(2)
+
+    @pl.loop(0, 2)
+    def _(x):
+        second_step(x)
+
+    wait(2 * 6 * 16 + 3 * (n_vel - 1), send_sem)
 
 
 def solution(mesh):
@@ -306,16 +417,17 @@
                 pltpu.VMEM(block, jnp.float32),
                 pltpu.VMEM(block, jnp.float32),
                 pltpu.VMEM(block, jnp.float32),
-                pltpu.VMEM((2, 8, LANES), jnp.float32),
-                pltpu.VMEM((2, n_vel, 8, LANES), jnp.float32),
+                pltpu.VMEM((3, 8, LANES), jnp.float32),
+                pltpu.VMEM((3, n_vel, 8, LANES), jnp.float32),
                 pltpu.VMEM((LANES, LANES), jnp.float32),
                 pltpu.VMEM((LANES, LANES), jnp.float32),
-                pltpu.VMEM((2 * (6 * 16 + n_vel - 1), 8, LANES), jnp.float32),
+                pltpu.VMEM((2 * 6 * 16 + 3 * (n_vel - 1), 8, LANES), jnp.float32),
                 pltpu.SemaphoreType.DMA,
                 pltpu.SemaphoreType.DMA,
-                pltpu.SemaphoreType.DMA((2,)),
-                pltpu.SemaphoreType.DMA((2,)),
-                pltpu.SemaphoreType.DMA((2,)),
+                pltpu.SemaphoreType.DMA((2, 2)),
+                pltpu.SemaphoreType.DMA((3,)),
+                pltpu.SemaphoreType.DMA((3,)),
+                pltpu.SemaphoreType.REGULAR((5,)),
             ],
             compiler_params=pltpu.CompilerParams(
                 collective_id=0,

time: 35.7 us -> 32.6 us (0.913)
  Pallas kernels: 34.8 us -> 31.6 us
    pallas_call x1, Pallas kernels: 34.8 us -> 31.6 us  [step(): pl.pallas_call(functools.partial(kernel, n_vel, n_x, n_y), out_shape=jax....]
where the time goes in v3:
time: 32.6 us; the launch traced here: 32.4 us
  Pallas kernels  31.6 us (97%)
  local copies, waits for them, and re-layouts  0.8 us (2%)
    pallas_call x1, Pallas kernels, step(): pl.pallas_call(functools.partial(kernel, n_vel, n_x, n_y), out_shape=jax....  31.6 us
    unnamed x1, local copies, waits for them, and re-layouts  0.8 us

profile of v3, /device:TPU:1, one launch (start us, length us, event | category | flops | bytes accessed | tf_op | source)
XLA Modules:
  0.0 32.4 jit_solution(13816178922213673758)
XLA Ops:
  0.0 31.6 %shard_map.17 = f32[8,8,2048]{2,1,0:T(8,128)S(1)} custom-call(f32[8,8,2048]{2,1,0:T(8,128)} %f_hbm.1), custom_call_target="tpu_custom_call" | custom-call | tf_op jit(solution)/shard_map/pallas_call | solution.py:408
  31.6 0.8 %copy.3 = f32[8,8,2048]{2,1,0:T(8,128)} copy(f32[8,8,2048]{2,1,0:T(8,128)S(1)} %shard_map.17) | data formatting | bytes 1048576

commit v4 on v3

--- a/solution.py
+++ b/solution.py
@@ -13,7 +13,6 @@
 UNIT = BOUND / KV
 WEIGHT = (2.0 * BOUND / KV) ** 3 * (2.0 * 3.141592653589793) ** (-1.5)
 MESH = pl.DeviceIdType.MESH
-HIGHEST = lax.Precision.HIGHEST
 NC = 64
 LANES = 128
 
@@ -21,35 +20,41 @@
 def functional_table():
     index = lax.broadcasted_iota(jnp.int32, (8, 1024), 1)
     row = lax.broadcasted_iota(jnp.int32, (8, 1024), 0)
-    b = (2 * (index // KV) + 1 - KV).astype(jnp.float32) * UNIT
-    e = (2 * (index % KV) + 1 - KV).astype(jnp.float32) * UNIT
-    one = jnp.ones_like(b)
+    b = (2 * (index // KV) + 1 - KV).astype(jnp.float32)
+    e = (2 * (index % KV) + 1 - KV).astype(jnp.float32)
     rest = b * b + e * e
-    rows = (one, b, e, b * b, b * e, e * e, b * rest, e * rest)
+    rows = (jnp.ones_like(b), b, e, b * b, b * e, e * e, b * rest, e * rest)
     table = jnp.zeros_like(b)
     for position, value in enumerate(rows):
         table = jnp.where(row == position, value, table)
-    return table * WEIGHT
+    high = table.astype(jnp.bfloat16)
+    low = (table - high.astype(jnp.float32)).astype(jnp.bfloat16)
+    return jnp.concatenate([high, low], axis=0)
 
 
 def partial_sums(cells, table, first):
     pieces = []
     size = cells.shape[0]
     for half in range(2):
-        value = lax.dot_general(
-            table,
-            cells[:, half * 1024 : (half + 1) * 1024],
-            (((1,), (1,)), ((), ())),
-            precision=HIGHEST,
-            preferred_element_type=jnp.float32,
-        )
+        rest = cells[:, half * 1024 : (half + 1) * 1024]
+        value = jnp.zeros((16, size), jnp.float32)
+        for part in range(3):
+            piece = rest.astype(jnp.bfloat16)
+            value = value + lax.dot_general(
+                table, piece, (((1,), (1,)), ((), ())),
+                preferred_element_type=jnp.float32,
+            )
+            if part < 2:
+                rest = rest - piece.astype(jnp.float32)
         before, after = first, NC - first - size
         if before:
             pieces.append(jnp.zeros((8, before), jnp.float32))
-        pieces.append(value)
+        pieces.append(value[:8] + value[8:])
         if after:
             pieces.append(jnp.zeros((8, after), jnp.float32))
-    return jnp.concatenate(pieces, axis=1)
+    row = lax.broadcasted_iota(jnp.int32, (8, LANES), 0)
+    scale = jnp.where(row == 0, 1.0, jnp.where(row < 3, UNIT, jnp.where(row < 6, UNIT**2, UNIT**3)))
+    return jnp.concatenate(pieces, axis=1) * (scale * WEIGHT)
 
 
 def cell_coefficients(sums_ref, n_vel):
@@ -105,10 +110,47 @@
     return d + 0.5 * (slope - slope_behind)
 
 
-def advance_row(x, field, low_ref, high_ref, coef_ref, sign, speeds_a, emit):
+def transport_tile(x, lanes, s, t, field, low_ref, high_ref, sign, speeds_a, along):
     row = lax.broadcasted_iota(jnp.int32, (8, LANES), 0)
     lane = lax.broadcasted_iota(jnp.int32, (8, LANES), 1)
     first, last = row == 0, row == 7
+    g = field[x + 2, :, lanes]
+    total = None
+    if "x" in along:
+        gm = field[x + 2 - sign, :, lanes]
+        gmm = field[x + 2 - 2 * sign, :, lanes]
+        gp = field[x + 2 + sign, :, lanes]
+        total = jnp.abs(speeds_a[t]) * DT * upwind(gm - gmm, gm, g, gp - g)
+    if "y" in along:
+        lo = low_ref[x, :, lanes]
+        hi = high_ref[x, :, lanes]
+        back = pltpu.roll(jnp.where(last, lo, g), 1, 0)
+        front = pltpu.roll(jnp.where(first, hi, g), 7, 0)
+        if s >= 4:
+            d = g - back
+            edge = lo - pltpu.roll(lo, 1, 0)
+            before = pltpu.roll(jnp.where(last, edge, d), 1, 0)
+            along_y = upwind(before, back, g, front - g)
+        else:
+            d = g - front
+            edge = hi - pltpu.roll(hi, 7, 0)
+            before = pltpu.roll(jnp.where(first, edge, d), 7, 0)
+            along_y = upwind(before, front, g, back - g)
+        cb = (2 * (lane // KV) - 3 + 8 * s - 28).astype(jnp.float32) * UNIT
+        part = jnp.abs(cb) * DT * along_y
+        total = part if total is None else total + part
+    return total
+
+
+def transport_row(x, field, low_ref, high_ref, sign, speeds_a, along, emit):
+    for s in range(8):
+        for t in range(2):
+            lanes = pl.ds((8 * t + s) * LANES, LANES)
+            emit(lanes, transport_tile(x, lanes, s, t, field, low_ref, high_ref, sign, speeds_a, along))
+
+
+def advance_row(x, field, coef_ref, speeds_a, transport, emit):
+    lane = lax.broadcasted_iota(jnp.int32, (8, LANES), 1)
     ce = (2 * (lane % KV) + 1 - KV).astype(jnp.float32) * UNIT
     lane_b = (2 * (lane // KV) - 3).astype(jnp.float32) * UNIT
     cell = coef_ref[pl.ds(pl.multiple_of(x * 8, 8), 8), :]
@@ -129,32 +171,12 @@
         gauss = jnp.exp(-square * half_t)
         ratio = square * inv_t
         heat = sb * qb + seq
-        vb = jnp.abs(cb) * DT
         for t in range(2):
             lanes = pl.ds((8 * t + s) * LANES, LANES)
             height, ratio_a, heat_a = level[t]
             relaxed = height * gauss * (1.0 + (heat + heat_a) * (ratio + ratio_a))
             g = field[x + 2, :, lanes]
-            gm = field[x + 2 - sign, :, lanes]
-            gmm = field[x + 2 - 2 * sign, :, lanes]
-            gp = field[x + 2 + sign, :, lanes]
-            along_x = upwind(gm - gmm, gm, g, gp - g)
-            lo = low_ref[x, :, lanes]
-            hi = high_ref[x, :, lanes]
-            back = pltpu.roll(jnp.where(last, lo, g), 1, 0)
-            front = pltpu.roll(jnp.where(first, hi, g), 7, 0)
-            if s >= 4:
-                d = g - back
-                edge = lo - pltpu.roll(lo, 1, 0)
-                before = pltpu.roll(jnp.where(last, edge, d), 1, 0)
-                along_y = upwind(before, back, g, front - g)
-            else:
-                d = g - front
-                edge = hi - pltpu.roll(hi, 7, 0)
-                before = pltpu.roll(jnp.where(first, edge, d), 7, 0)
-                along_y = upwind(before, front, g, back - g)
-            speed = jnp.abs(speeds_a[t]) * DT
-            emit(lanes, keep * g + relaxed - (speed * along_x + vb * along_y))
+            emit(lanes, keep * g + relaxed - transport(lanes, s, t))
 
 
 def kernel(
@@ -176,14 +198,16 @@
     top = jnp.logical_and(corner, v == 0)
 
     def rank_of(vel):
-        plain = 2 * fold(vel // 2, n_vel // 2) + 1 - lax.rem(vel, 2)
+        plain = 2 * (vel // 2) + 1 - lax.rem(vel, 2)
         in_corner = jnp.where(vel == 0, n_vel - 1, plain - jnp.where(plain > 1, 1, 0))
         return jnp.where(corner, in_corner, plain)
 
     def side_above(side, plain):
         there_x, there_y = side.get("sx", sx), side.get("sy", sy)
+        wrap = jnp.abs(there_x - sx) == n_x - 1
         there = jnp.logical_and(jnp.logical_and(there_x == 0, there_y == 0), v == 0)
-        return jnp.logical_and(jnp.logical_or(plain, there), jnp.logical_not(top))
+        moved = jnp.logical_and(jnp.logical_or(plain, there), jnp.logical_not(top))
+        return jnp.where(wrap, plain, moved)
 
     y_rank = fold(sy, n_y)
     sides = tuple(
@@ -201,6 +225,8 @@
     order = sorted(range(1, n_vel), key=lambda j: -min(j, n_vel - j))
     others = [{"vel": lax.rem(v + j, n_vel)} for j in order]
 
+    load = pltpu.make_async_copy(f_hbm, field.at[pl.ds(2, 8)], in_sem)
+    load.start()
     barrier = pltpu.get_barrier_semaphore()
     for to, above, _ in sides:
         @pl.when(above)
@@ -212,9 +238,6 @@
         def _(to=to):
             pl.semaphore_signal(barrier, inc=1, device_id=to, device_id_type=MESH)
 
-    load = pltpu.make_async_copy(f_hbm, field.at[pl.ds(2, 8)], in_sem)
-    load.start()
-
     table = functional_table()
     speeds_a = [
         (4 * v + 2 * t + 1 - KV).astype(jnp.float32) * UNIT for t in range(2)
@@ -231,19 +254,20 @@
             total.at[pl.ds(0, tiles)], total.at[pl.ds(0, tiles)], sem
         ).wait()
 
-    def send_x(source, stage, rising):
+    def send_x(source, dest, stage, rising):
+        base = 2 if source is dest else 0
         to, sem = (up_x, x_sem.at[stage, 0]) if rising else (down_x, x_sem.at[stage, 1])
-        far, near = ((8, 0), (9, 1)) if rising else ((2, 10), (2, 10))
+        far, near = ((6, 0), (7, 1)) if rising else ((0, 10), (0, 10))
 
         @pl.when(upward if rising else downward)
         def _():
             src, dst = far
-            send(source.at[pl.ds(src, 2)], source.at[pl.ds(dst, 2)], sem, to)
+            send(source.at[pl.ds(src + base, 2)], dest.at[pl.ds(dst, 2)], sem, to)
 
         @pl.when(downward if rising else upward)
         def _():
             src, dst = near
-            send(source.at[pl.ds(src, 1)], source.at[pl.ds(dst, 1)], sem, to)
+            send(source.at[pl.ds(src + base, 1)], dest.at[pl.ds(dst, 1)], sem, to)
 
     def arrive_x(stage, rising):
         sem = x_sem.at[stage, 0 if rising else 1]
@@ -288,21 +312,57 @@
         wait(n_vel - 1, sum_sem.at[slot])
         write_coefficients(sums.at[slot], rows, coef, n_vel)
 
-    def first_step(x):
+    def tiles(x, along, second):
+        source, below, above = (field2, low2, high2) if second else (field, low, high)
+
+        def transport(lanes, s, t):
+            return transport_tile(x, lanes, s, t, source, below, above, sign, speeds_a, along)
+
+        return transport
+
+    def first_transport(x):
         def emit(lanes, value):
             field2[x + 2, :, lanes] = value
 
-        advance_row(x, field, low, high, coef, sign, speeds_a, emit)
-
-    def second_step(x):
+        transport_row(x, field, low, high, sign, speeds_a, "xy", emit)
+
+    def first_step(x, along="xy"):
+        def emit(lanes, value):
+            field2[x + 2, :, lanes] = value
+
+        def kept(lanes, s, t):
+            return field2[x + 2, :, lanes]
+
+        transport = tiles(x, along, False) if along else kept
+        advance_row(x, field, coef, speeds_a, transport, emit)
+
+    def first_step_along_x(x):
+        def emit(lanes, value):
+            field2[x + 2, :, lanes] = field2[x + 2, :, lanes] - value
+
+        transport_row(x, field, low, high, sign, speeds_a, "x", emit)
+
+    def finish(x, transport):
         def emit(lanes, value):
             out_v[x, :, lanes] = 0.5 * (field[x + 2, :, lanes] + value)
 
-        advance_row(x, field2, low2, high2, coef, sign, speeds_a, emit)
+        advance_row(x, field2, coef, speeds_a, transport, emit)
+
+    def finish_along_x(x):
+        def emit(lanes, value):
+            out_v[x, :, lanes] = out_v[x, :, lanes] - 0.5 * value
+
+        transport_row(x, field2, low2, high2, sign, speeds_a, "x", emit)
+
+    def second_transport(x):
+        def emit(lanes, value):
+            out_v[x, :, lanes] = value
+
+        transport_row(x, field2, low2, high2, sign, speeds_a, "xy", emit)
 
     begin = (
-        lambda: send_x(field, 0, True),
-        lambda: send_x(field, 0, False),
+        lambda: send_x(f_hbm, field, 0, True),
+        lambda: send_x(f_hbm, field, 0, False),
         lambda: send_y(field, low, y_sem.at[0], 0, 8, True),
         lambda: send_y(field, high, y_sem.at[0], 0, 8, False),
     )
@@ -312,6 +372,9 @@
     def _():
         pl.semaphore_wait(barrier, entered)
 
+    for start, below in zip(begin[:2], lower[:2]):
+        pl.when(below)(start)
+
     for (to, _, index), below in zip(sides, lower):
         @pl.when(below)
         def _(to=to, index=index):
@@ -323,7 +386,7 @@
             pl.semaphore_signal(go.at[4], inc=1, device_id=to, device_id_type=MESH)
 
     load.wait()
-    for start, below in zip(begin, lower):
+    for start, below in zip(begin[2:], lower[2:]):
         pl.when(below)(start)
 
     own_sums(field, 0, 0, 8)
@@ -351,33 +414,43 @@
         def _(to=to):
             send(mine.at[0], sums.at[0, v], sum_sem.at[0], to)
 
+    begin_above(1)
     wait(3 * 16, y_sem.at[0])
+    arrive_x(0, False)
+
+    @pl.loop(6, 8)
+    def _(x):
+        first_transport(x)
+
     gather(0)
+
+    @pl.loop(6, 8)
+    def _(x):
+        first_step(x, None)
+
+    send_x(field2, field2, 1, True)
 
     @pl.loop(2, 6)
     def _(x):
         first_step(x)
 
-    begin_above(1)
-    arrive_x(0, False)
-
-    @pl.loop(6, 8)
-    def _(x):
-        first_step(x)
-
-    send_x(field2, 1, True)
     own_sums(field2, 1, 2, 6)
     share(1)
     exchange_y(field2, low2, high2, y_sem.at[1], 2, 6)
-    arrive_x(0, True)
 
     @pl.loop(0, 2)
     def _(x):
-        first_step(x)
+        first_step(x, "y")
+
+    arrive_x(0, True)
+
+    @pl.loop(0, 2)
+    def _(x):
+        first_step_along_x(x)
 
     own_sums(field2, 2, 0, 2)
     share(2)
-    send_x(field2, 1, False)
+    send_x(field2, field2, 1, False)
     exchange_y(field2, low2, high2, y_sem.at[2], 0, 2)
 
     wait(36, y_sem.at[1])
@@ -386,15 +459,37 @@
 
     @pl.loop(2, 8)
     def _(x):
-        second_step(x)
+        finish(x, tiles(x, "xy", True))
 
     wait(12, y_sem.at[2])
-    arrive_x(1, True)
-    gather(2)
-
-    @pl.loop(0, 2)
-    def _(x):
-        second_step(x)
+
+    @pl.when(upward)
+    def _():
+        gather(2)
+
+        @pl.loop(0, 2)
+        def _(x):
+            finish(x, tiles(x, "y", True))
+
+        arrive_x(1, True)
+
+        @pl.loop(0, 2)
+        def _(x):
+            finish_along_x(x)
+
+    @pl.when(downward)
+    def _():
+        arrive_x(1, True)
+
+        @pl.loop(0, 2)
+        def _(x):
+            second_transport(x)
+
+        gather(2)
+
+        @pl.loop(0, 2)
+        def _(x):
+            finish(x, lambda lanes, s, t: out_v[x, :, lanes])
 
     wait(2 * 6 * 16 + 3 * (n_vel - 1), send_sem)
 

time: 32.6 us -> 32.2 us (0.988)
    pallas_call x1, Pallas kernels: 31.6 us -> 31.3 us  [step(): pl.pallas_call(functools.partial(kernel, n_vel, n_x, n_y), out_shape=jax....]
where the time goes in v4:
time: 32.2 us; the launch traced here: 32.1 us
  Pallas kernels  31.3 us (97%)
  local copies, waits for them, and re-layouts  0.8 us (2%)
    pallas_call x1, Pallas kernels, step(): pl.pallas_call(functools.partial(kernel, n_vel, n_x, n_y), out_shape=jax....  31.3 us
    unnamed x1, local copies, waits for them, and re-layouts  0.8 us

profile of v4, /device:TPU:1, one launch (start us, length us, event | category | flops | bytes accessed | tf_op | source)
XLA Modules:
  0.0 32.1 jit_solution(14190576356013379149)
XLA Ops:
  0.0 31.3 %shard_map.17 = f32[8,8,2048]{2,1,0:T(8,128)S(1)} custom-call(f32[8,8,2048]{2,1,0:T(8,128)} %f_hbm.1), custom_call_target="tpu_custom_call" | custom-call | tf_op jit(solution)/shard_map/pallas_call | solution.py:503
  31.3 0.8 %copy.3 = f32[8,8,2048]{2,1,0:T(8,128)} copy(f32[8,8,2048]{2,1,0:T(8,128)S(1)} %shard_map.17) | data formatting | bytes 1048576

commit v5 on v4

--- a/solution.py
+++ b/solution.py
@@ -149,7 +149,7 @@
             emit(lanes, transport_tile(x, lanes, s, t, field, low_ref, high_ref, sign, speeds_a, along))
 
 
-def advance_row(x, field, coef_ref, speeds_a, transport, emit):
+def advance_row(x, field, coef_ref, speeds_a, transport, emit, shift=2):
     lane = lax.broadcasted_iota(jnp.int32, (8, LANES), 1)
     ce = (2 * (lane % KV) + 1 - KV).astype(jnp.float32) * UNIT
     lane_b = (2 * (lane // KV) - 3).astype(jnp.float32) * UNIT
@@ -175,12 +175,12 @@
             lanes = pl.ds((8 * t + s) * LANES, LANES)
             height, ratio_a, heat_a = level[t]
             relaxed = height * gauss * (1.0 + (heat + heat_a) * (ratio + ratio_a))
-            g = field[x + 2, :, lanes]
+            g = field[x + shift, :, lanes]
             emit(lanes, keep * g + relaxed - transport(lanes, s, t))
 
 
 def kernel(
-    n_vel, n_x, n_y, f_hbm, out_v,
+    n_vel, n_x, n_y, f_hbm, out_v, edge_rows, edge_coef,
     field, field2, low, high, low2, high2, mine, sums, rows, coef, total,
     in_sem, send_sem, x_sem, y_sem, sum_sem, go,
 ):
@@ -198,7 +198,7 @@
     top = jnp.logical_and(corner, v == 0)
 
     def rank_of(vel):
-        plain = 2 * (vel // 2) + 1 - lax.rem(vel, 2)
+        plain = vel + 1 - 2 * lax.rem(vel, 2)
         in_corner = jnp.where(vel == 0, n_vel - 1, plain - jnp.where(plain > 1, 1, 0))
         return jnp.where(corner, in_corner, plain)
 
@@ -224,6 +224,8 @@
     rank = rank_of(v)
     order = sorted(range(1, n_vel), key=lambda j: -min(j, n_vel - j))
     others = [{"vel": lax.rem(v + j, n_vel)} for j in order]
+    other_above = [rank_of(to["vel"]) > rank for to in others]
+    other_below = [jnp.logical_not(above) for above in other_above]
 
     load = pltpu.make_async_copy(f_hbm, field.at[pl.ds(2, 8)], in_sem)
     load.start()
@@ -233,8 +235,8 @@
         def _(to=to):
             pl.semaphore_signal(barrier, inc=1, device_id=to, device_id_type=MESH)
 
-    for to in others:
-        @pl.when(rank_of(to["vel"]) > rank)
+    for to, above in zip(others, other_above):
+        @pl.when(above)
         def _(to=to):
             pl.semaphore_signal(barrier, inc=1, device_id=to, device_id_type=MESH)
 
@@ -310,7 +312,7 @@
 
     def gather(slot):
         wait(n_vel - 1, sum_sem.at[slot])
-        write_coefficients(sums.at[slot], rows, coef, n_vel)
+        write_coefficients(sums.at[slot], rows, edge_coef if slot == 2 else coef, n_vel)
 
     def tiles(x, along, second):
         source, below, above = (field2, low2, high2) if second else (field, low, high)
@@ -348,17 +350,17 @@
 
         advance_row(x, field2, coef, speeds_a, transport, emit)
 
-    def finish_along_x(x):
+    def add_along_x(x):
         def emit(lanes, value):
-            out_v[x, :, lanes] = out_v[x, :, lanes] - 0.5 * value
+            out_v[x, :, lanes] = out_v[x, :, lanes] + value
 
         transport_row(x, field2, low2, high2, sign, speeds_a, "x", emit)
 
-    def second_transport(x):
+    def second_transport(x, along):
         def emit(lanes, value):
             out_v[x, :, lanes] = value
 
-        transport_row(x, field2, low2, high2, sign, speeds_a, "xy", emit)
+        transport_row(x, field2, low2, high2, sign, speeds_a, along, emit)
 
     begin = (
         lambda: send_x(f_hbm, field, 0, True),
@@ -380,8 +382,8 @@
         def _(to=to, index=index):
             pl.semaphore_signal(go.at[index], inc=1, device_id=to, device_id_type=MESH)
 
-    for to in others:
-        @pl.when(rank_of(to["vel"]) < rank)
+    for to, below in zip(others, other_below):
+        @pl.when(below)
         def _(to=to):
             pl.semaphore_signal(go.at[4], inc=1, device_id=to, device_id_type=MESH)
 
@@ -390,8 +392,8 @@
         pl.when(below)(start)
 
     own_sums(field, 0, 0, 8)
-    for to in others:
-        @pl.when(rank_of(to["vel"]) < rank)
+    for to, below in zip(others, other_below):
+        @pl.when(below)
         def _(to=to):
             send(mine.at[0], sums.at[0, v], sum_sem.at[0], to)
 
@@ -409,8 +411,8 @@
     def _():
         pl.semaphore_wait(go.at[4], n_vel - 1 - rank)
 
-    for to in others:
-        @pl.when(rank_of(to["vel"]) > rank)
+    for to, above in zip(others, other_above):
+        @pl.when(above)
         def _(to=to):
             send(mine.at[0], sums.at[0, v], sum_sem.at[0], to)
 
@@ -463,19 +465,23 @@
 
     wait(12, y_sem.at[2])
 
+    @pl.loop(0, 2)
+    def _(x):
+        edge_rows[x] = field2[x + 2]
+        edge_rows[x + 2] = field[x + 2]
+
     @pl.when(upward)
     def _():
-        gather(2)
-
         @pl.loop(0, 2)
         def _(x):
-            finish(x, tiles(x, "y", True))
-
+            second_transport(x, "y")
+
+        gather(2)
         arrive_x(1, True)
 
         @pl.loop(0, 2)
         def _(x):
-            finish_along_x(x)
+            add_along_x(x)
 
     @pl.when(downward)
     def _():
@@ -483,15 +489,32 @@
 
         @pl.loop(0, 2)
         def _(x):
-            second_transport(x)
+            second_transport(x, "xy")
 
         gather(2)
 
-        @pl.loop(0, 2)
-        def _(x):
-            finish(x, lambda lanes, s, t: out_v[x, :, lanes])
+    for t in range(2):
+        edge_coef[pl.ds(NC + 8 * t, 8), :] = jnp.full((8, LANES), speeds_a[t])
 
     wait(2 * 6 * 16 + 3 * (n_vel - 1), send_sem)
+
+
+def finish_kernel(value, edge_rows, edge_coef, out_hbm, done, sem):
+    rest = pltpu.make_async_copy(value.at[pl.ds(2, 6)], out_hbm.at[pl.ds(2, 6)], sem.at[0])
+    rest.start()
+    speeds_a = [edge_coef[NC + 8 * t : NC + 8 * t + 8, :] for t in range(2)]
+    for x in range(2):
+        def emit(lanes, new):
+            done[x, :, lanes] = 0.5 * (edge_rows[x + 2, :, lanes] + new)
+
+        advance_row(
+            x, edge_rows, edge_coef, speeds_a,
+            lambda lanes, s, t: value[x, :, lanes], emit, 0,
+        )
+    last = pltpu.make_async_copy(done, out_hbm.at[pl.ds(0, 2)], sem.at[1])
+    last.start()
+    last.wait()
+    rest.wait()
 
 
 def solution(mesh):
@@ -500,11 +523,15 @@
     def step(table):
         block = table.shape
         table = pltpu.with_memory_space_constraint(table, pltpu.HBM)
-        return pl.pallas_call(
+        parts = pl.pallas_call(
             functools.partial(kernel, n_vel, n_x, n_y),
-            out_shape=jax.ShapeDtypeStruct(block, jnp.float32),
+            out_shape=[
+                jax.ShapeDtypeStruct(block, jnp.float32),
+                jax.ShapeDtypeStruct((4, 8, 2048), jnp.float32),
+                jax.ShapeDtypeStruct((LANES, LANES), jnp.float32),
+            ],
             in_specs=[pl.BlockSpec(memory_space=pltpu.HBM)],
-            out_specs=pl.BlockSpec(memory_space=pltpu.VMEM),
+            out_specs=[pl.BlockSpec(memory_space=pltpu.VMEM)] * 3,
             scratch_shapes=[
                 pltpu.VMEM((12, 8, 2048), jnp.float32),
                 pltpu.VMEM((12, 8, 2048), jnp.float32),
@@ -530,6 +557,17 @@
                 vmem_limit_bytes=16 * 1024 * 1024,
             ),
         )(table)
+        return pl.pallas_call(
+            finish_kernel,
+            out_shape=jax.ShapeDtypeStruct(block, jnp.float32),
+            in_specs=[pl.BlockSpec(memory_space=pltpu.VMEM)] * 3,
+            out_specs=pl.BlockSpec(memory_space=pl.ANY),
+            scratch_shapes=[
+                pltpu.VMEM((2, 8, 2048), jnp.float32),
+                pltpu.SemaphoreType.DMA((2,)),
+            ],
+            compiler_params=pltpu.CompilerParams(vmem_limit_bytes=16 * 1024 * 1024),
+        )(*parts)
 
     return jax.shard_map(
         step,

time: 32.2 us -> 32 us (level)
  local copies, waits for them, and re-layouts: 0.8 us -> 0 us
  Pallas kernels: 31.3 us -> 31.8 us
    unnamed x1 -> x0, local copies, waits for them, and re-layouts: 0.8 us -> none
    pallas_call x1 -> x2, Pallas kernels: 31.3 us -> 31.8 us  [the longest x1 31 us: step(): pl.pallas_call(functools.partial(kernel, n_vel, n_x, n_y), out_shape=[jax...]
where the time goes in v5:
time: 32 us; the launch traced here: 31.8 us
  Pallas kernels  31.8 us (99%)
    pallas_call x1, Pallas kernels, step(): pl.pallas_call(functools.partial(kernel, n_vel, n_x, n_y), out_shape=[jax...  31 us
    pallas_call x1, Pallas kernels, step(): pl.pallas_call(finish_kernel, out_shape=jax.ShapeDtypeStruct(block, jnp.f...  0.83 us

profile of v5, /device:TPU:1, one launch (start us, length us, event | category | flops | bytes accessed | tf_op | source)
XLA Modules:
  0.0 31.8 jit_solution(15303938749168763733)
XLA Ops:
  0.0 31.0 %shard_map.17 = (f32[8,8,2048]{2,1,0:T(8,128)S(1)}, f32[4,8,2048]{2,1,0:T(8,128)S(1)}, f32[128,128]{1,0:T(8,128)S(1)}) custom-call(f32[8,8,2048]{2,1,0:T(8,128)} %f_hbm.1), custom_call_target="tpu_custom_call" | custom-call | tf_op jit(solution)/shard_map/pallas_call | solution.py:526
  31.0 0.8 %shard_map.18 = f32[8,8,2048]{2,1,0:T(8,128)} custom-call(f32[8,8,2048]{2,1,0:T(8,128)S(1)} %get-tuple-element.8.value, f32[4,8,2048]{2,1,0:T(8,128)S(1)} %get-tuple-element.9.edge_rows, f32[128,128]{1,0:T(8,128)S(1)} %get-tuple-element.10.edge_coef), custom_call_target="tpu_custom_call" | custom-call | tf_op jit(solution)/shard_map/pallas_call | solution.py:560
